TPU v7x, 32 devices: a whole 2x2x4 slice. The times are simulated.
32 devices in a mesh: expert: 16 (over z, y, x), tok: 2 (over core).
Axes of the slice: x: 2, y: 2, z: 4, core: 2. Of those that a mesh axis runs over, the one named last changes fastest.
Arguments:
- tokens: bfloat16 [2048, 3584], P(('expert', 'tok')), may hold values from -6 to 6
- routes: int32 [2048, 8], P(('expert', 'tok')), may hold values from 0 to 15, all different within a row; in each aligned block of 64 rows (0 to 63, 64 to 127, ...) at most 36 rows name the same one
- gates: float32 [2048, 8], P(('expert', 'tok')), may hold values from 0.05 to 1
- upstream: bfloat16 [2048, 3584], P(('expert', 'tok')), may hold values from -6 to 6
- w_up: bfloat16 [16, 3584, 1024], P('expert', None, 'tok'), may hold values from -0.09375 to 0.09375
- w_down: bfloat16 [16, 1024, 3584], P('expert', 'tok'), may hold values from -0.1875 to 0.1875
Outputs:
- mixed: bfloat16 [2048, 3584], P(('expert', 'tok'))
- d_tokens: bfloat16 [2048, 3584], P(('expert', 'tok'))
- d_gates: float32 [2048, 8], P(('expert', 'tok'))
- grad_up: bfloat16 [16, 3584, 1024], P('expert', None, 'tok')
- grad_down: bfloat16 [16, 1024, 3584], P('expert', 'tok')
Inputs may be any that keep to these rules, and one draw needn't show every extreme that they name: `routes`: each token names 8 different experts. At most 36 of the 64 tokens of one device name the same expert, and in every draw the tokens of some device name some expert exactly 36 times.
All inputs are finite; a program needn't handle non-finite values.
Results may differ from a plain program's by a relative error of at most 0.0065.
Values may be sent and summed in bfloat16 or wider, within the bound.
A program may use at most 192 MiB of HBM per device.

v0:
```python
import jax
import jax.numpy as jnp
from jax import lax
from jax.sharding import PartitionSpec as P

GELU_C = 0.7978845608028654
GELU_A = 0.044715


def gelu_value(hidden):
    inner_arg = GELU_C * (hidden + GELU_A * hidden * hidden * hidden)
    return 0.5 * hidden * (1.0 + jnp.tanh(inner_arg))


def gelu_slope(hidden):
    tangent = jnp.tanh(GELU_C * (hidden + GELU_A * hidden * hidden * hidden))
    return 0.5 * (1.0 + tangent) + 0.5 * hidden * (1.0 - tangent * tangent) * GELU_C * (
        1.0 + 3.0 * GELU_A * hidden * hidden
    )


def expert_rows(rows_x, rows_grad, up_local, down_local):
    hidden = jnp.dot(rows_x, up_local, preferred_element_type=jnp.float32)
    active = gelu_value(hidden).astype(jnp.bfloat16)
    out_part = jnp.dot(active, down_local, preferred_element_type=jnp.float32)
    d_active = lax.dot_general(
        rows_grad, down_local, (((1,), (1,)), ((), ())), preferred_element_type=jnp.float32
    )
    d_hidden = (d_active * gelu_slope(hidden)).astype(jnp.bfloat16)
    dx_part = lax.dot_general(
        d_hidden, up_local, (((1,), (1,)), ((), ())), preferred_element_type=jnp.float32
    )
    grad_down = lax.dot_general(
        active, rows_grad, (((0,), (0,)), ((), ())), preferred_element_type=jnp.float32
    )
    grad_up = lax.dot_general(
        rows_x, d_hidden, (((0,), (0,)), ((), ())), preferred_element_type=jnp.float32
    )
    return (out_part, dx_part, grad_up, grad_down)


def routed_shards(tokens, routes, gates, upstream, w_up, w_down):
    tok_rows, feature_width = tokens.shape
    top_count = routes.shape[1]
    owners = lax.axis_size("expert")
    pair_count = lax.axis_size("tok")
    capacity = tok_rows * top_count // owners + max(1, tok_rows * top_count // (8 * owners))
    assigned = routes.reshape(-1)
    labels = jnp.arange(owners, dtype=jnp.int32)
    onehot = (assigned[:, None] == labels[None, :]).astype(jnp.int32)
    earlier = jnp.cumsum(onehot, axis=0) - onehot
    slot_rank = jnp.sum(earlier * onehot, axis=1)
    slot_of = assigned * capacity + slot_rank
    slot_ids = jnp.arange(owners * capacity, dtype=jnp.int32)
    matches = (slot_of[None, :] == slot_ids[:, None]).astype(jnp.int32)
    filled = jnp.sum(matches, axis=1) > 0
    source = jnp.sum(matches * jnp.arange(assigned.shape[0], dtype=jnp.int32)[None, :], axis=1)
    token_ids = source // top_count
    send_x = jnp.where(filled[:, None], tokens[token_ids], jnp.zeros((), jnp.bfloat16))
    gate_rows = jnp.where(filled, gates.reshape(-1)[source], jnp.zeros((), jnp.float32))
    send_grad = (gate_rows[:, None] * upstream[token_ids].astype(jnp.float32)).astype(jnp.bfloat16)
    send_x = send_x.reshape(owners, capacity, feature_width)
    send_grad = send_grad.reshape(owners, capacity, feature_width)
    recv_x, recv_grad = (
        lax.all_to_all(send_x, "expert", split_axis=0, concat_axis=0, tiled=True),
        lax.all_to_all(send_grad, "expert", split_axis=0, concat_axis=0, tiled=True),
    )
    both_x, both_grad = (
        lax.all_gather(recv_x[None], "tok", axis=0, tiled=True),
        lax.all_gather(recv_grad[None], "tok", axis=0, tiled=True),
    )
    rows_x = both_x.reshape(-1, feature_width)
    rows_grad = both_grad.reshape(-1, feature_width)
    out_part, dx_part, grad_up, grad_down = expert_rows(rows_x, rows_grad, w_up[0], w_down[0])
    shaped_out = out_part.reshape(pair_count, owners, capacity, feature_width)
    shaped_dx = dx_part.reshape(pair_count, owners, capacity, feature_width)
    summed_out, summed_dx = (
        lax.psum_scatter(shaped_out, "tok", scatter_dimension=0, tiled=True),
        lax.psum_scatter(shaped_dx, "tok", scatter_dimension=0, tiled=True),
    )
    home_out, home_dx = (
        lax.all_to_all(
            summed_out[0].astype(jnp.bfloat16), "expert", split_axis=0, concat_axis=0, tiled=True
        ),
        lax.all_to_all(
            summed_dx[0].astype(jnp.bfloat16), "expert", split_axis=0, concat_axis=0, tiled=True
        ),
    )
    out_pairs = (
        home_out.reshape(owners * capacity, feature_width)[slot_of]
        .reshape(tok_rows, top_count, feature_width)
        .astype(jnp.float32)
    )
    dx_pairs = (
        home_dx.reshape(owners * capacity, feature_width)[slot_of]
        .reshape(tok_rows, top_count, feature_width)
        .astype(jnp.float32)
    )
    mixed_out = jnp.sum(gates[:, :, None] * out_pairs, axis=1).astype(jnp.bfloat16)
    d_gates = jnp.sum(upstream.astype(jnp.float32)[:, None, :] * out_pairs, axis=2)
    d_tokens = jnp.sum(dx_pairs, axis=1).astype(jnp.bfloat16)
    return (
        mixed_out,
        d_tokens,
        d_gates,
        grad_up.astype(jnp.bfloat16)[None],
        grad_down.astype(jnp.bfloat16)[None],
    )


def dense_shards(tokens, routes, gates, upstream, w_up, w_down):
    tok_rows, width = tokens.shape
    owners = lax.axis_size("expert")
    half = w_up.shape[2]
    swap = ((0, 1), (1, 0))
    up_local, down_local = (w_up[0], w_down[0])
    up_full = jnp.concatenate([up_local, lax.ppermute(up_local, "tok", swap)], axis=1)
    down_full = jnp.concatenate([down_local, lax.ppermute(down_local, "tok", swap)], axis=0)
    named = routes[:, :, None] == jnp.arange(owners, dtype=jnp.int32)
    gate_of = jnp.sum(jnp.where(named, gates[:, :, None], 0.0), axis=1)
    gate = lax.all_to_all(gate_of.T, "expert", split_axis=0, concat_axis=0, tiled=True)
    gate = gate.reshape(-1)[:, None]
    all_x = lax.all_gather(tokens, "expert", axis=0, tiled=True)
    all_u = lax.all_gather(upstream, "expert", axis=0, tiled=True)
    hidden = jnp.dot(all_x, up_full, preferred_element_type=jnp.float32)
    gated = (gate * gelu_value(hidden)).astype(jnp.bfloat16)
    mixed_part = jnp.dot(gated, down_full, preferred_element_type=jnp.float32)
    mixed = lax.psum_scatter(
        mixed_part.astype(jnp.bfloat16), "expert", scatter_dimension=0, tiled=True
    )
    back = lax.dot_general(
        all_u, down_full, (((1,), (1,)), ((), ())), preferred_element_type=jnp.float32
    )
    inner = jnp.sum(gelu_value(hidden) * back, axis=1)
    d_hidden = (gate * back * gelu_slope(hidden)).astype(jnp.bfloat16)
    dx_part = lax.dot_general(
        d_hidden, up_full, (((1,), (1,)), ((), ())), preferred_element_type=jnp.float32
    )
    d_tokens = lax.psum_scatter(
        dx_part.astype(jnp.bfloat16), "expert", scatter_dimension=0, tiled=True
    )
    home = lax.all_to_all(
        inner.reshape(owners, tok_rows), "expert", split_axis=0, concat_axis=0, tiled=True
    )
    d_gates = jnp.sum(jnp.where(named, home.T[:, None, :], 0.0), axis=2)

    def outer(rows, columns):
        return lax.dot_general(
            rows, columns, (((0,), (0,)), ((), ())), preferred_element_type=jnp.float32
        )

    down_far = outer(gated[:, half:], all_u).astype(jnp.bfloat16)
    up_far = outer(all_x, d_hidden[:, half:]).astype(jnp.bfloat16)
    down_near = outer(gated[:, :half], all_u)
    up_near = outer(all_x, d_hidden[:, :half])
    grad_down = down_near + lax.ppermute(down_far, "tok", swap).astype(jnp.float32)
    grad_up = up_near + lax.ppermute(up_far, "tok", swap).astype(jnp.float32)
    return (
        mixed,
        d_tokens,
        d_gates,
        grad_up.astype(jnp.bfloat16)[None],
        grad_down.astype(jnp.bfloat16)[None],
    )


def shards(tokens, routes, gates, upstream, w_up, w_down):
    dense = 2 * routes.shape[1] >= lax.axis_size("expert") and lax.axis_size("tok") == 2
    body = dense_shards if dense else routed_shards
    return body(tokens, routes, gates, upstream, w_up, w_down)


def solution(mesh):
    return jax.shard_map(
        shards,
        mesh=mesh,
        in_specs=(
            P(("expert", "tok"), None),
            P(("expert", "tok"), None),
            P(("expert", "tok"), None),
            P(("expert", "tok"), None),
            P("expert", None, "tok"),
            P("expert", "tok", None),
        ),
        out_specs=(
            P(("expert", "tok"), None),
            P(("expert", "tok"), None),
            P(("expert", "tok"), None),
            P("expert", None, "tok"),
            P("expert", "tok", None),
        ),
        check_vma=False,
    )
```

profile of v0, /device:TPU:10, one launch (start us, length us, event | category | flops | bytes accessed | tf_op | source)
XLA Modules:
  0.0 600.3 jit_solution(6524580034297987019)
XLA Ops:
  7.2 0.0 all-gather.3.cloned.1.call-start
  7.2 0.7 all-gather.3.cloned.1.call-update
  7.9 0.0 all-gather.5.cloned.1.call-start
  7.9 0.7 all-gather.5.cloned.1.call-update
  8.6 0.0 reduce-scatter.5.cloned.1.call-start
  8.7 0.1 collective-permute-start
  8.8 0.5 collective-permute-start.1
  9.3 6.2 %collective-permute-done = bf16[3584,512]{1,0:T(8,128)(2,1)} collective-permute-done((bf16[3584,512]{1,0:T(8,128)(2,1)}, bf16[3584,512]{1,0:T(8,128)(2,1)}, u32[]{:S(2)}, u32[]{:S(2)}) %collective-permute-start) | collective-permute-done | bytes 3670048 | tf_op jit(solution)/shard_map/ppermute | solution.py:117
  15.5 98.8 %all-gather.3.cloned.1.call-done = bf16[1024,3584]{1,0:T(8,128)(2,1)} async-done(((bf16[64,3584]{1,0:T(8,128)(2,1)}), bf16[1024,3584]{1,0:T(8,128)(2,1)}) %all-gather.3.cloned.1.call-update) | async-done | bytes 7340048 | tf_op jit(solution)/shard_map/all_gather | solution.py:123
  114.3 13.6 %fusion.4 = f32[1024,1024]{1,0:T(8,128)} fusion(bf16[1024,3584]{1,0:T(8,128)(2,1)} %all-gather.3.cloned.1.call-done, bf16[3584,512]{1,0:T(8,128)(2,1)} %collective-permute-done, bf16[3584,512]{1,0:T(8,128)(2,1)} %bitcast.60), kind=kOutput, calls=%fused_computation.14 | convolution fusion | flops 7530872832 | bytes 18874368 | tf_op jit(solution)/shard_map/dot_general | solution.py:125
  127.9 0.0 copy-start.2
  127.9 0.0 copy-start.3
  127.9 0.0 collective-permute-done.1
  127.9 90.8 %all-gather.5.cloned.1.call-done = bf16[1024,3584]{1,0:T(8,128)(2,1)} async-done(((bf16[64,3584]{1,0:T(8,128)(2,1)}), bf16[1024,3584]{1,0:T(8,128)(2,1)}) %all-gather.5.cloned.1.call-update) | async-done | bytes 7340048 | tf_op jit(solution)/shard_map/all_gather | solution.py:124
  218.7 15.0 %fusion.12 = (f32[1024]{0:T(1024)S(1)}, f32[1024,1024]{1,0:T(8,128)}) fusion(f32[1024,1024]{1,0:T(8,128)} %fusion.4, bf16[1024,3584]{1,0:T(8,128)(2,1)} %all-gather.5.cloned.1.call-done, bf16[512,3584]{1,0:T(8,128)(2,1)} %collective-permute-done.1, bf16[512,3584]{1,0:T(8,128)(2,1)} %bitcast.63), kind=kOutput, calls=%fused_computation.24 | convolution fusion | flops 7541357568 | bytes 23072768 | tf_op jit(solution)/shard_map/dot_general | solution.py:131
  233.7 0.1 all_to_all.16
  233.7 10.0 %all_to_all.21 = f32[16,1,64]{2,1,0:T(1,128)S(1)} all-to-all(f32[16,1,64]{2,1,0:T(1,128)S(1)} %bitcast.56), channel_id=1, replica_groups=mesh['expert'=16,'tok'=2] {'expert'}, dimensions={0} | all-to-all | bytes 8192 | tf_op jit(solution)/shard_map/all_to_all | solution.py:142
  243.8 0.0 copy-done.2
  243.8 0.0 copy-done.3
  243.8 0.6 select_reduce_fusion
  244.4 9.8 %all_to_all.22 = f32[16,1,64]{2,1,0:T(1,128)S(1)} all-to-all(f32[16,1,64]{2,1,0:T(1,128)S(1)} %bitcast.55), channel_id=1, replica_groups=mesh['expert'=16,'tok'=2] {'expert'}, dimensions={0} | all-to-all | bytes 8192 | tf_op jit(solution)/shard_map/all_to_all | solution.py:121
  254.2 0.5 broadcast.46
  254.7 0.7 reduce.3
  255.4 0.1 mul.75
  255.5 0.0 copy-start.4
  255.5 5.6 fusion.11
  261.1 0.0 copy-start
  261.1 1.3 copy-done
  262.4 0.0 copy-done.4
  262.4 12.0 %convolution_convert_fusion = bf16[1024,3584]{1,0:T(8,128)(2,1)} fusion(bf16[1024,1024]{0,1:T(8,128)(2,1)S(1)} %get-tuple-element.27, bf16[3584,512]{1,0:T(8,128)(2,1)} %collective-permute-done, bf16[3584,512]{1,0:T(8,128)(2,1)S(1)} %bitcast.61), kind=kOutput, calls=%fused_computation | convolution fusion | flops 7534542848 | bytes 16777216 | tf_op jit(solution)/shard_map/dot_general | solution.py:136
  274.4 0.0 reduce-scatter.5.cloned.1.call-update
  274.4 0.3 reduce-scatter.3.cloned.1.call-start
  274.6 13.0 %convolution_convert_fusion.1 = bf16[1024,3584]{1,0:T(8,128)(2,1)} fusion(bf16[1024,1024]{0,1:T(8,128)(2,1)S(1)} %get-tuple-element.28, bf16[512,3584]{1,0:T(8,128)(2,1)} %collective-permute-done.1, bf16[512,3584]{1,0:T(8,128)(2,1)} %bitcast.64), kind=kOutput, calls=%fused_computation.1 | convolution fusion | flops 7534542848 | bytes 16777216 | tf_op jit(solution)/shard_map/dot_general | solution.py:127
  287.7 0.0 reduce-scatter.3.cloned.1.call-update
  287.7 0.0 slice-start
  287.7 7.5 %fusion.1 = bf16[3584,512]{0,1:T(8,128)(2,1)S(1)} fusion(bf16[1024,3584]{1,0:T(8,128)(2,1)} %all-gather.3.cloned.1.call-done, bf16[1024,1024]{0,1:T(8,128)(2,1)} %copy-done), kind=kOutput, calls=%fused_computation.11 | convolution fusion | flops 3759931392 | bytes 12058624 | tf_op jit(solution)/shard_map/dot_general | solution.py:148
  295.3 0.0 copy-start.1
  295.3 0.0 slice-start.1
  295.3 0.1 collective-permute-start.2
  295.4 8.7 %convolution_convert_fusion.2 = bf16[512,3584]{1,0:T(8,128)(2,1)} fusion(bf16[1024,3584]{1,0:T(8,128)(2,1)} %all-gather.5.cloned.1.call-done, bf16[1024,1024]{0,1:T(8,128)(2,1)S(1)} %get-tuple-element.28), kind=kOutput, calls=%fused_computation.9 | convolution fusion | flops 3759931392 | bytes 12058624 | tf_op jit(solution)/shard_map/dot_general | solution.py:148
  304.0 0.3 collective-permute-start.3
  304.4 0.0 collective-permute-done.2
  304.4 0.0 slice-done
  304.4 0.0 copy-done.1
  304.4 0.0 slice-done.1
  304.4 5.4 fusion.2
  309.8 5.9 copy.25
  315.7 0.0 collective-permute-done.3
  315.7 9.1 %fusion.14 = bf16[1,512,3584]{2,1,0:T(8,128)(2,1)} fusion(bf16[512,3584]{1,0:T(8,128)(2,1)} %collective-permute-done.3, bf16[1024,3584]{1,0:T(8,128)(2,1)} %all-gather.5.cloned.1.call-done, bf16[1024,1024]{0,1:T(8,128)(2,1)S(1)} %get-tuple-element.28), kind=kOutput, calls=%fused_computation.28 | convolution fusion | flops 3763601408 | bytes 15728640 | tf_op jit(solution)/shard_map/dot_general | solution.py:148
  324.8 107.0 %reduce-scatter.5.cloned.1.call-done = bf16[64,3584]{1,0:T(8,128)(2,1)} async-done(((bf16[1024,3584]{1,0:T(8,128)(2,1)}), bf16[64,3584]{1,0:T(8,128)(2,1)}) %reduce-scatter.5.cloned.1.call-update) | async-done | bytes 458768 | tf_op jit(solution)/shard_map/reduce_scatter | solution.py:139
  431.8 161.9 %reduce-scatter.3.cloned.1.call-done = bf16[64,3584]{1,0:T(8,128)(2,1)} async-done(((bf16[1024,3584]{1,0:T(8,128)(2,1)}), bf16[64,3584]{1,0:T(8,128)(2,1)}) %reduce-scatter.3.cloned.1.call-update) | async-done | bytes 458768 | tf_op jit(solution)/shard_map/reduce_scatter | solution.py:128
  (1 shorter events, 0.0 us)
Async XLA Ops:
  7.2 107.2 %all-gather.3.cloned.1.call-start = ((), (), s32[]{:S(2)}) async-start(), calls=%async_computation.4 | async-start | bytes 7798784 | tf_op jit(solution)/shard_map/all_gather | solution.py:123
  7.9 210.8 %all-gather.5.cloned.1.call-start = ((), (), s32[]{:S(2)}) async-start(), calls=%async_computation.6 | async-start | bytes 7798784 | tf_op jit(solution)/shard_map/all_gather | solution.py:124
  8.6 423.2 %reduce-scatter.5.cloned.1.call-start = ((), (), s32[]{:S(2)}) async-start(), calls=%async_computation.7 | async-start | bytes 7798784 | tf_op jit(solution)/shard_map/reduce_scatter | solution.py:139
  8.7 6.8 %collective-permute-start = (bf16[3584,512]{1,0:T(8,128)(2,1)}, bf16[3584,512]{1,0:T(8,128)(2,1)}, u32[]{:S(2)}, u32[]{:S(2)}) collective-permute-start(bf16[3584,512]{1,0:T(8,128)(2,1)} %bitcast.59), channel_id=1, source_target_pairs={{0,1},{1,0},{2,3},{3,2},{4,5},{5,4},{6,7},{7,6},{8,9},{9,8},{10,11... | collective-permute-start | bytes 11010056 | tf_op jit(solution)/shard_map/ppermute | solution.py:117
  8.8 119.1 %collective-permute-start.1 = (bf16[512,3584]{1,0:T(8,128)(2,1)}, bf16[512,3584]{1,0:T(8,128)(2,1)}, u32[]{:S(2)}, u32[]{:S(2)}) collective-permute-start(bf16[512,3584]{1,0:T(8,128)(2,1)} %bitcast.62), channel_id=1, source_target_pairs={{0,1},{1,0},{2,3},{3,2},{4,5},{5,4},{6,7},{7,6},{8,9},{9,8},{10,11... | collective-permute-start | bytes 11010056 | tf_op jit(solution)/shard_map/ppermute | solution.py:118
  127.9 115.9 %copy-start.2 = (s32[64,8]{0,1:T(8,128)S(1)}, s32[64,8]{0,1:T(8,128)}, u32[]{:S(2)}) copy-start(s32[64,8]{0,1:T(8,128)} %param.7) | copy-start | bytes 6148
  127.9 115.9 %copy-start.3 = (f32[64,8]{0,1:T(8,128)S(1)}, f32[64,8]{0,1:T(8,128)}, u32[]{:S(2)}) copy-start(f32[64,8]{0,1:T(8,128)} %param.8) | copy-start | bytes 6148
  255.5 6.9 %copy-start.4 = (bf16[1,3584,512]{2,1,0:T(8,128)(2,1)S(1)}, bf16[1,3584,512]{2,1,0:T(8,128)(2,1)}, u32[]{:S(2)}) copy-start(bf16[1,3584,512]{2,1,0:T(8,128)(2,1)} %param.10) | copy-start | bytes 11010052
  261.1 1.3 copy-start
  274.4 319.4 %reduce-scatter.3.cloned.1.call-start = ((), (), s32[]{:S(2)}) async-start(), calls=%async_computation.5 | async-start | bytes 7798784 | tf_op jit(solution)/shard_map/reduce_scatter | solution.py:128
  287.7 16.6 %slice-start = ((s8[7340032]{0:T(1024)(128)(4,1)}), s8[4194304]{0:T(1024)(128)(4,1)S(1)}, s32[]{:S(2)}) async-start(s8[7340032]{0:T(1024)(128)(4,1)} %bitcast.57), calls=%async_computation.8 | async-start | bytes 8388608
  295.3 9.1 %copy-start.1 = (bf16[1024,1024]{0,1:T(8,128)(2,1)S(1)}, bf16[1024,1024]{0,1:T(8,128)(2,1)}, u32[]{:S(2)}) copy-start(bf16[1024,1024]{0,1:T(8,128)(2,1)} %copy-done) | copy-start | bytes 6291460
  295.3 9.1 %slice-start.1 = ((s8[7340032]{0:T(1024)(128)(4,1)}), s8[3145728]{0:T(1024)(128)(4,1)S(1)}, s32[]{:S(2)}) async-start(s8[7340032]{0:T(1024)(128)(4,1)} %bitcast.57), calls=%async_computation.9 | async-start | bytes 6291456
  295.3 9.1 %collective-permute-start.2 = (bf16[3584,512]{0,1:T(8,128)(2,1)S(1)}, bf16[3584,512]{0,1:T(8,128)(2,1)S(1)}, u32[]{:S(2)}, u32[]{:S(2)}) collective-permute-start(bf16[3584,512]{0,1:T(8,128)(2,1)S(1)} %fusion.1), channel_id=1, source_target_pairs={{0,1},{1,0},{2,3},{3,2},{4,5},{5,4},{6,7},{7,6},{8,9},{9,8},{10,11... | collective-permute-start | bytes 11010056 | tf_op jit(solution)/shard_map/ppermute | solution.py:157
  304.0 11.7 %collective-permute-start.3 = (bf16[512,3584]{1,0:T(8,128)(2,1)}, bf16[512,3584]{1,0:T(8,128)(2,1)}, u32[]{:S(2)}, u32[]{:S(2)}) collective-permute-start(bf16[512,3584]{1,0:T(8,128)(2,1)} %convolution_convert_fusion.2), channel_id=1, source_target_pairs={{0,1},{1,0},{2,3},{3,2},{4,5},{5,4},{6,7},{7,6},{8,9},{9,8},{10,11... | collective-permute-start | bytes 11010056 | tf_op jit(solution)/shard_map/ppermute | solution.py:156
Sparse Core Ops, SparseCore 0:
  10.7 103.6 all-gather.2
  117.0 101.6 all-gather.4
  274.5 157.2 reduce-scatter.4
  434.6 159.1 reduce-scatter.2
where the time goes:
time: 601 us; the launch traced here: 600 us
  waiting for transfers between devices  466 us (78%)
  matrix products  84.3 us (14%)
  blocking collectives  19.9 us (3%)
  between operations  13.9 us (2%)
  local copies, waits for them, and re-layouts  7.92 us (1%)
  other arithmetic  6.87 us (1%)
    reduce_scatter x1, waiting for transfers between devices, dense_shards(): lax.psum_scatter(mixed_part.astype(jnp.bfloat16), 'expert', scatter_dimen...  162 us
    reduce_scatter x1, waiting for transfers between devices, dense_shards(): lax.psum_scatter(dx_part.astype(jnp.bfloat16), 'expert', scatter_dimensio...  107 us
    all_gather x1, waiting for transfers between devices, dense_shards(): all_x = lax.all_gather(tokens, 'expert', axis=0, tiled=True)  98.8 us
    all_gather x1, waiting for transfers between devices, dense_shards(): all_u = lax.all_gather(upstream, 'expert', axis=0, tiled=True)  90.8 us
    dot_general x4, matrix products, outer(): lax.dot_general(rows, columns, (((0,), (0,)), ((), ())), preferred_elemen...  30.7 us
    dot_general x1, matrix products, dense_shards(): lax.dot_general(all_u, down_full, (((1,), (1,)), ((), ())), preferred_ele...  15 us
    dot_general x1, matrix products, dense_shards(): hidden = jnp.dot(all_x, up_full, preferred_element_type=jnp.float32)  13.6 us
    dot_general x1, matrix products, dense_shards(): mixed_part = jnp.dot(gated, down_full, preferred_element_type=jnp.float32)  13 us
  transfers between devices with their start and end apart: 8, of which 5 were waited for; matrix products, arithmetic and copies ran while one was open for 11% of the time, Pallas kernels for 0%

commit v1 on v0

--- a/solution.py
+++ b/solution.py
@@ -120,7 +120,14 @@
     gate_of = jnp.sum(jnp.where(named, gates[:, :, None], 0.0), axis=1)
     gate = lax.all_to_all(gate_of.T, "expert", split_axis=0, concat_axis=0, tiled=True)
     gate = gate.reshape(-1)[:, None]
-    all_x = lax.all_gather(tokens, "expert", axis=0, tiled=True)
+    ways, here = (lax.axis_size("expert"), lax.axis_index("expert"))
+    all_x, reach = (tokens, 1)
+    while reach < ways:
+        theirs = lax.ppermute(all_x, "expert", [(d, d ^ reach) for d in range(ways)])
+        mine_first = jnp.concatenate([all_x, theirs], axis=0)
+        theirs_first = jnp.concatenate([theirs, all_x], axis=0)
+        all_x = jnp.where(here & reach == 0, mine_first, theirs_first)
+        reach = 2 * reach
     all_u = lax.all_gather(upstream, "expert", axis=0, tiled=True)
     hidden = jnp.dot(all_x, up_full, preferred_element_type=jnp.float32)
     gated = (gate * gelu_value(hidden)).astype(jnp.bfloat16)

time: 601 us -> 702 us (1.17)
  waiting for transfers between devices: 466 us -> 555 us
  other arithmetic: 6.87 us -> 15.1 us
  local copies, waits for them, and re-layouts: 7.92 us -> 0.67 us
    ppermute x0 -> x4, waiting for transfers between devices: none -> 282 us  [dense_shards(): lax.ppermute(all_x, 'expert', [(d, d ^ reach) for d in range(ways)])]
    all_gather x1 -> x0, waiting for transfers between devices: 98.8 us -> none  [dense_shards(): all_x = lax.all_gather(tokens, 'expert', axis=0, tiled=True)]
    all_gather x1, waiting for transfers between devices: 90.8 us -> 0.02 us  [dense_shards(): all_u = lax.all_gather(upstream, 'expert', axis=0, tiled=True)]
    unnamed x15 -> x12, local copies, waits for them, and re-layouts: 7.26 us -> 0.02 us
    select_n x0 -> x3, other arithmetic: none -> 7.19 us  [dense_shards(): all_x = jnp.where(here & reach == 0, mine_first, theirs_first)]
  transfers between devices with their start and end apart: 8 -> 11, of which waited for: 5 -> 7; matrix products, arithmetic and copies ran while one was open for 11% -> 10% of each run, Pallas kernels for 0% -> 0%
where the time goes in v1:
time: 702 us
  waiting for transfers between devices  555 us (79%)
  matrix products  87.4 us (12%)
  blocking collectives  22.6 us (3%)
  other arithmetic  15.1 us (2%)
  between operations  13.8 us (2%)
    ppermute x4, waiting for transfers between devices, dense_shards(): lax.ppermute(all_x, 'expert', [(d, d ^ reach) for d in range(ways)])  282 us
    reduce_scatter x1, waiting for transfers between devices, dense_shards(): lax.psum_scatter(mixed_part.astype(jnp.bfloat16), 'expert', scatter_dimen...  162 us
    reduce_scatter x1, waiting for transfers between devices, dense_shards(): lax.psum_scatter(dx_part.astype(jnp.bfloat16), 'expert', scatter_dimensio...  110 us
    dot_general x4, matrix products, outer(): lax.dot_general(rows, columns, (((0,), (0,)), ((), ())), preferred_elemen...  33.3 us
    dot_general x1, matrix products, dense_shards(): lax.dot_general(all_u, down_full, (((1,), (1,)), ((), ())), preferred_ele...  14.8 us
    dot_general x1, matrix products, dense_shards(): hidden = jnp.dot(all_x, up_full, preferred_element_type=jnp.float32)  14.6 us
  transfers between devices with their start and end apart: 11, of which 7 were waited for; matrix products, arithmetic and copies ran while one was open for 10% of the time, Pallas kernels for 0%

profile of v1, /device:TPU:10, one launch (start us, length us, event | category | flops | bytes accessed | tf_op | source)
XLA Modules:
  0.0 701.7 jit_solution(11287858426783208429)
XLA Ops:
  7.2 0.0 all-gather.2.cloned.1.call-start
  7.2 0.7 all-gather.2.cloned.1.call-update
  7.9 0.0 reduce-scatter.5.cloned.1.call-start
  7.9 0.6 collective-permute-start
  8.5 11.9 %collective-permute-done = bf16[64,3584]{1,0:T(8,128)(2,1)S(1)} collective-permute-done((bf16[64,3584]{1,0:T(8,128)(2,1)}, bf16[64,3584]{1,0:T(8,128)(2,1)S(1)}, u32[]{:S(2)}, u32[]{:S(2)}) %collective-permute-start) | collective-permute-done | bytes 458784 | tf_op jit(solution)/shard_map/ppermute | solution.py:126
  20.5 1.4 maximum_select_fusion.3
  21.9 1.6 collective-permute-start.1
  23.4 25.4 %collective-permute-done.1 = bf16[128,3584]{1,0:T(8,128)(2,1)} collective-permute-done((bf16[128,3584]{1,0:T(8,128)(2,1)S(1)}, bf16[128,3584]{1,0:T(8,128)(2,1)}, u32[]{:S(2)}, u32[]{:S(2)}) %collective-permute-start.1) | collective-permute-done | bytes 917536 | tf_op jit(solution)/shard_map/ppermute | solution.py:126
  48.8 1.9 maximum_select_fusion.2
  50.8 0.6 collective-permute-start.2
  51.3 0.0 collective-permute-start.4
  51.3 88.8 %collective-permute-done.2 = bf16[256,3584]{1,0:T(8,128)(2,1)} collective-permute-done((bf16[256,3584]{1,0:T(8,128)(2,1)S(1)}, bf16[256,3584]{1,0:T(8,128)(2,1)}, u32[]{:S(2)}, u32[]{:S(2)}) %collective-permute-start.2) | collective-permute-done | bytes 1835040 | tf_op jit(solution)/shard_map/ppermute | solution.py:126
  140.1 3.9 maximum_select_fusion.1
  144.0 3.3 collective-permute-start.3
  147.3 0.0 collective-permute-start.5
  147.3 0.0 collective-permute-done.4
  147.4 155.6 %collective-permute-done.3 = bf16[512,3584]{1,0:T(8,128)(2,1)} collective-permute-done((bf16[512,3584]{1,0:T(8,128)(2,1)}, bf16[512,3584]{1,0:T(8,128)(2,1)}, u32[]{:S(2)}, u32[]{:S(2)}) %collective-permute-start.3) | collective-permute-done | bytes 3670048 | tf_op jit(solution)/shard_map/ppermute | solution.py:126
  302.9 14.6 %fusion.2 = f32[1024,1024]{0,1:T(8,128)} fusion(bf16[3584,512]{1,0:T(8,128)(2,1)} %collective-permute-done.4, bf16[3584,512]{1,0:T(8,128)(2,1)} %bitcast.33, bf16[512,3584]{1,0:T(8,128)(2,1)} %collective-permute-done.3, bf16[512,3584]{1,0:T(8,128)(2,1)} %maximum_select_fusion.1, pred[]{:T(512)S(6)} %eq.28), kind=kOutput, calls=%fused_computation.13 | convolution fusion | flops 7563902976 | bytes 18874368 | tf_op jit(solution)/shard_map/dot_general | solution.py:132
  317.5 0.0 copy-start.1
  317.5 0.0 copy-start.2
  317.5 0.0 collective-permute-done.5
  317.5 0.0 all-gather.2.cloned.1.call-done
  317.6 14.8 %fusion.10 = (f32[1024]{0:T(1024)S(1)}, f32[1024,1024]{1,0:T(8,128)}) fusion(f32[1024,1024]{0,1:T(8,128)} %fusion.2, bf16[1024,3584]{1,0:T(8,128)(2,1)} %all-gather.2.cloned.1.call-done, bf16[512,3584]{1,0:T(8,128)(2,1)} %collective-permute-done.5, bf16[512,3584]{1,0:T(8,128)(2,1)} %bitcast.4), kind=kOutput, calls=%fused_computation.23 | convolution fusion | flops 7541357568 | bytes 23072768 | tf_op jit(solution)/shard_map/dot_general | solution.py:138
  332.4 0.1 all_to_all.16
  332.5 12.8 %all_to_all.21 = f32[16,1,64]{2,1,0:T(1,128)S(1)} all-to-all(f32[16,1,64]{2,1,0:T(1,128)S(1)} %bitcast.29), channel_id=1, replica_groups=mesh['expert'=16,'tok'=2] {'expert'}, dimensions={0} | all-to-all | bytes 8192 | tf_op jit(solution)/shard_map/all_to_all | solution.py:149
  345.3 0.0 copy-done.1
  345.3 0.0 copy-done.2
  345.3 0.6 select_reduce_fusion
  345.9 9.8 %all_to_all.22 = f32[16,1,64]{2,1,0:T(1,128)S(1)} all-to-all(f32[16,1,64]{2,1,0:T(1,128)S(1)} %bitcast.28), channel_id=1, replica_groups=mesh['expert'=16,'tok'=2] {'expert'}, dimensions={0} | all-to-all | bytes 8192 | tf_op jit(solution)/shard_map/all_to_all | solution.py:121
  355.7 0.5 broadcast.46
  356.3 0.7 reduce.3
  356.9 0.1 mul.75
  357.0 0.0 copy-start.3
  357.0 6.6 fusion.9
  363.6 0.0 copy-done.3
  363.6 12.0 %convolution_convert_fusion = bf16[1024,3584]{1,0:T(8,128)(2,1)} fusion(bf16[1024,1024]{0,1:T(8,128)(2,1)S(1)} %get-tuple-element.7, bf16[3584,512]{1,0:T(8,128)(2,1)} %collective-permute-done.4, bf16[3584,512]{1,0:T(8,128)(2,1)S(1)} %bitcast.34), kind=kOutput, calls=%fused_computation | convolution fusion | flops 7534542848 | bytes 16777216 | tf_op jit(solution)/shard_map/dot_general | solution.py:143
  375.7 0.0 reduce-scatter.5.cloned.1.call-update
  375.7 0.3 reduce-scatter.3.cloned.1.call-start
  375.9 12.7 %convolution_convert_fusion.1 = bf16[1024,3584]{1,0:T(8,128)(2,1)} fusion(bf16[1024,1024]{0,1:T(8,128)(2,1)} %get-tuple-element.8, bf16[512,3584]{1,0:T(8,128)(2,1)} %collective-permute-done.5, bf16[512,3584]{1,0:T(8,128)(2,1)} %bitcast.4), kind=kOutput, calls=%fused_computation.1 | convolution fusion | flops 7534542848 | bytes 16777216 | tf_op jit(solution)/shard_map/dot_general | solution.py:134
  388.6 0.0 reduce-scatter.3.cloned.1.call-update
  388.6 0.0 slice-start
  388.7 9.4 %convolution_convert_fusion.2 = bf16[512,3584]{1,0:T(8,128)(2,1)} fusion(bf16[1024,3584]{1,0:T(8,128)(2,1)} %all-gather.2.cloned.1.call-done, bf16[1024,1024]{0,1:T(8,128)(2,1)} %get-tuple-element.8), kind=kOutput, calls=%fused_computation.9 | convolution fusion | flops 3759931392 | bytes 12058624 | tf_op jit(solution)/shard_map/dot_general | solution.py:155
  398.0 0.0 copy-start
  398.0 0.0 slice-start.1
  398.0 0.0 collective-permute-start.7
  398.1 9.1 %convolution_convert_fusion.3 = bf16[3584,512]{1,0:T(8,128)(2,1)} fusion(bf16[1024,1024]{0,1:T(8,128)(2,1)S(1)} %get-tuple-element.7, bf16[512,3584]{1,0:T(8,128)(2,1)} %collective-permute-done.3, bf16[512,3584]{1,0:T(8,128)(2,1)} %maximum_select_fusion.1, pred[]{:T(512)S(6)} %eq.28), kind=kOutput, calls=%fused_computation.10 | convolution fusion | flops 3792961536 | bytes 12058625 | tf_op jit(solution)/shard_map/dot_general | solution.py:155
  407.2 0.5 collective-permute-start.6
  407.7 0.0 collective-permute-done.7
  407.7 0.0 slice-done
  407.7 0.0 copy-done
  407.7 0.0 slice-done.1
  407.7 5.4 fusion.11
  413.1 0.8 collective-permute-done.6
  413.9 9.3 %fusion = bf16[1,3584,512]{2,1,0:T(8,128)(2,1)} fusion(bf16[3584,512]{1,0:T(8,128)(2,1)S(1)} %collective-permute-done.6, bf16[1024,1024]{0,1:T(8,128)(2,1)S(1)} %get-tuple-element.7, bf16[512,3584]{1,0:T(8,128)(2,1)} %collective-permute-done.3, bf16[512,3584]{1,0:T(8,128)(2,1)} %maximum_select_fusion.1, pred[]{:T(512)S(6)} %eq.28), kind=kOutput, calls=%fused_computation.11 | convolution fusion | flops 3796631552 | bytes 15728641 | tf_op jit(solution)/shard_map/dot_general | solution.py:155
  423.3 109.9 %reduce-scatter.5.cloned.1.call-done = bf16[64,3584]{1,0:T(8,128)(2,1)} async-done(((bf16[1024,3584]{1,0:T(8,128)(2,1)}), bf16[64,3584]{1,0:T(8,128)(2,1)}) %reduce-scatter.5.cloned.1.call-update) | async-done | bytes 458768 | tf_op jit(solution)/shard_map/reduce_scatter | solution.py:146
  533.1 162.1 %reduce-scatter.3.cloned.1.call-done = bf16[64,3584]{1,0:T(8,128)(2,1)} async-done(((bf16[1024,3584]{1,0:T(8,128)(2,1)}), bf16[64,3584]{1,0:T(8,128)(2,1)}) %reduce-scatter.3.cloned.1.call-update) | async-done | bytes 458768 | tf_op jit(solution)/shard_map/reduce_scatter | solution.py:135
  (1 shorter events, 0.0 us)
Async XLA Ops:
  7.2 310.4 %all-gather.2.cloned.1.call-start = ((), (), s32[]{:S(2)}) async-start(), calls=%async_computation.5 | async-start | bytes 7798784 | tf_op jit(solution)/shard_map/all_gather | solution.py:131
  7.9 525.2 %reduce-scatter.5.cloned.1.call-start = ((), (), s32[]{:S(2)}) async-start(), calls=%async_computation.6 | async-start | bytes 7798784 | tf_op jit(solution)/shard_map/reduce_scatter | solution.py:146
  7.9 12.5 %collective-permute-start = (bf16[64,3584]{1,0:T(8,128)(2,1)}, bf16[64,3584]{1,0:T(8,128)(2,1)S(1)}, u32[]{:S(2)}, u32[]{:S(2)}) collective-permute-start(bf16[64,3584]{1,0:T(8,128)(2,1)} %param.6), channel_id=1, source_target_pairs={{0,2},{2,0},{4,6},{6,4},{8,10},{10,8},{12,14},{14,12},{16,18},{18,... | collective-permute-start | bytes 1376264 | tf_op jit(solution)/shard_map/ppermute | solution.py:126
  21.9 27.0 %collective-permute-start.1 = (bf16[128,3584]{1,0:T(8,128)(2,1)S(1)}, bf16[128,3584]{1,0:T(8,128)(2,1)}, u32[]{:S(2)}, u32[]{:S(2)}) collective-permute-start(bf16[128,3584]{1,0:T(8,128)(2,1)S(1)} %maximum_select_fusion.3), channel_id=1, source_target_pairs={{0,4},{2,6},{4,0},{6,2},{8,12},{10,14},{12,8},{14,10},{16,20},{18,... | collective-permute-start | bytes 2752520 | tf_op jit(solution)/shard_map/ppermute | solution.py:126
  50.8 89.3 %collective-permute-start.2 = (bf16[256,3584]{1,0:T(8,128)(2,1)S(1)}, bf16[256,3584]{1,0:T(8,128)(2,1)}, u32[]{:S(2)}, u32[]{:S(2)}) collective-permute-start(bf16[256,3584]{1,0:T(8,128)(2,1)S(1)} %maximum_select_fusion.2), channel_id=1, source_target_pairs={{0,8},{2,10},{4,12},{6,14},{8,0},{10,2},{12,4},{14,6},{16,24},{18,... | collective-permute-start | bytes 5505032 | tf_op jit(solution)/shard_map/ppermute | solution.py:126
  51.3 96.0 %collective-permute-start.4 = (bf16[3584,512]{1,0:T(8,128)(2,1)}, bf16[3584,512]{1,0:T(8,128)(2,1)}, u32[]{:S(2)}, u32[]{:S(2)}) collective-permute-start(bf16[3584,512]{1,0:T(8,128)(2,1)} %bitcast.32), channel_id=1, source_target_pairs={{0,1},{1,0},{2,3},{3,2},{4,5},{5,4},{6,7},{7,6},{8,9},{9,8},{10,11... | collective-permute-start | bytes 11010056 | tf_op jit(solution)/shard_map/ppermute | solution.py:117
  144.0 158.9 %collective-permute-start.3 = (bf16[512,3584]{1,0:T(8,128)(2,1)}, bf16[512,3584]{1,0:T(8,128)(2,1)}, u32[]{:S(2)}, u32[]{:S(2)}) collective-permute-start(bf16[512,3584]{1,0:T(8,128)(2,1)} %maximum_select_fusion.1), channel_id=1, source_target_pairs={{0,16},{2,18},{4,20},{6,22},{8,24},{10,26},{12,28},{14,30},{16,0},... | collective-permute-start | bytes 11010056 | tf_op jit(solution)/shard_map/ppermute | solution.py:126
  147.3 170.2 %collective-permute-start.5 = (bf16[512,3584]{1,0:T(8,128)(2,1)}, bf16[512,3584]{1,0:T(8,128)(2,1)}, u32[]{:S(2)}, u32[]{:S(2)}) collective-permute-start(bf16[512,3584]{1,0:T(8,128)(2,1)} %bitcast.4), channel_id=1, source_target_pairs={{0,1},{1,0},{2,3},{3,2},{4,5},{5,4},{6,7},{7,6},{8,9},{9,8},{10,11... | collective-permute-start | bytes 11010056 | tf_op jit(solution)/shard_map/ppermute | solution.py:118
  317.5 27.8 %copy-start.1 = (s32[64,8]{0,1:T(8,128)S(1)}, s32[64,8]{0,1:T(8,128)}, u32[]{:S(2)}) copy-start(s32[64,8]{0,1:T(8,128)} %param.7) | copy-start | bytes 6148
  317.5 27.8 %copy-start.2 = (f32[64,8]{0,1:T(8,128)S(1)}, f32[64,8]{0,1:T(8,128)}, u32[]{:S(2)}) copy-start(f32[64,8]{0,1:T(8,128)} %param.8) | copy-start | bytes 6148
  357.0 6.6 copy-start.3
  375.7 319.5 %reduce-scatter.3.cloned.1.call-start = ((), (), s32[]{:S(2)}) async-start(), calls=%async_computation.4 | async-start | bytes 7798784 | tf_op jit(solution)/shard_map/reduce_scatter | solution.py:135
  388.6 19.1 %slice-start = ((s8[7340032]{0:T(1024)(128)(4,1)}), s8[4194304]{0:T(1024)(128)(4,1)S(1)}, s32[]{:S(2)}) async-start(s8[7340032]{0:T(1024)(128)(4,1)} %bitcast.30), calls=%async_computation.7 | async-start | bytes 8388608
  398.0 9.7 %copy-start = (bf16[1024,1024]{0,1:T(8,128)(2,1)S(1)}, bf16[1024,1024]{0,1:T(8,128)(2,1)}, u32[]{:S(2)}) copy-start(bf16[1024,1024]{0,1:T(8,128)(2,1)} %get-tuple-element.8) | copy-start | bytes 6291460
  398.0 9.7 %slice-start.1 = ((s8[7340032]{0:T(1024)(128)(4,1)}), s8[3145728]{0:T(1024)(128)(4,1)S(1)}, s32[]{:S(2)}) async-start(s8[7340032]{0:T(1024)(128)(4,1)} %bitcast.30), calls=%async_computation.8 | async-start | bytes 6291456
  398.0 9.6 %collective-permute-start.7 = (bf16[512,3584]{1,0:T(8,128)(2,1)}, bf16[512,3584]{1,0:T(8,128)(2,1)S(1)}, u32[]{:S(2)}, u32[]{:S(2)}) collective-permute-start(bf16[512,3584]{1,0:T(8,128)(2,1)} %convolution_convert_fusion.2), channel_id=1, source_target_pairs={{0,1},{1,0},{2,3},{3,2},{4,5},{5,4},{6,7},{7,6},{8,9},{9,8},{10,11... | collective-permute-start | bytes 11010056 | tf_op jit(solution)/shard_map/ppermute | solution.py:163
  407.2 6.7 collective-permute-start.6
Sparse Core Ops, SparseCore 0:
  10.7 132.1 all-gather.1
  375.8 157.2 reduce-scatter.4
  536.0 159.1 reduce-scatter.2
